TPU v7x, 32 devices: a whole 2x2x4 slice. The times are simulated.
32 devices in a mesh: pipe: 4 (over x, core), expert: 4 (over z), tensor: 2 (over y).
Axes of the slice: x: 2, y: 2, z: 4, core: 2. Of those that a mesh axis runs over, the one named last changes fastest.
Arguments:
- stream: bfloat16 [2, 4, 64, 7168], P(None, 'pipe', 'expert', 'tensor'), may hold values from -6 to 6
- expert_ids: int32 [2, 4, 64, 2], P(None, 'pipe', 'expert'), may hold values from 0 to 3, all different within a row; in each aligned block of 16 rows (0 to 15, 16 to 31, ..., all dimensions but the last counted through in order) at most 12 rows name the same one
- norm_gain: float32 [4, 7168], P('pipe', 'tensor'), may hold values from 0.1 to 1.9
- router: float32 [4, 7168, 4], P('pipe', 'tensor'), may hold values from -0.0625 to 0.0625
- w_up: bfloat16 [4, 7168, 1024], P('expert', 'tensor'), may hold values from -0.0625 to 0.0625
- w_down: bfloat16 [4, 1024, 7168], P('expert', None, 'tensor'), may hold values from -0.1875 to 0.1875
Outputs:
- result: bfloat16 [2, 4, 64, 7168], P(None, 'pipe', 'expert', 'tensor')
Inputs may be any that keep to these rules, and one draw needn't show every extreme that they name: `expert_ids`: each token names 2 different experts. Among the 16 tokens of one direction held by one index of the expert axis at one section, at most 12 name any one expert, and in every draw some expert is named by exactly 12 of them.
All inputs are finite; a program needn't handle non-finite values.
Results may differ from a plain program's by a relative error of at most 0.0065.
Values may be sent and summed in bfloat16 or wider, within the bound.
A program may use at most 64 MiB of HBM per device.

v0:
```python
import jax
import jax.numpy as jnp
from jax import lax
from jax.sharding import PartitionSpec as P

norm_eps = 1e-06
route_scale = 2.5


def shifted(x, axis, by):
    size = lax.axis_size(axis)
    return lax.ppermute(x, axis, [(i, (i + by) % size) for i in range(size)])


def shards(stream, expert_ids, norm_gain, router, w_up, w_down):
    ahead = shifted(stream[0], "pipe", 1)
    behind = shifted(stream[1], "pipe", -1)
    arrived = jnp.concatenate([ahead, behind], axis=0).astype(jnp.float32)
    tok_rows = arrived.shape[1]
    quarter = arrived.shape[2]
    width = float(quarter * lax.axis_size("tensor"))
    scaled = arrived * norm_gain[0]
    squares = jnp.sum(arrived * arrived, axis=-1)
    highest = lax.Precision.HIGHEST
    total_sq = lax.psum(squares, "tensor")
    inverse = lax.rsqrt(total_sq / width + norm_eps)
    normed = scaled * inverse[..., None]
    logits = lax.psum(jnp.einsum("dtc,ce->dte", normed, router[0], precision=highest), "tensor")
    chosen = expert_ids[:, 0]
    fanout = chosen.shape[2]
    experts = router.shape[2]
    capacity = 3 * tok_rows * fanout // (2 * experts)
    picked = jnp.take_along_axis(logits, chosen, axis=-1)
    scores = jax.nn.sigmoid(picked)
    gates = route_scale * scores / jnp.sum(scores, axis=-1, keepdims=True)
    onehot = (chosen[..., None] == jnp.arange(experts, dtype=jnp.int32)).astype(jnp.int32)
    onehot = onehot.reshape(2, tok_rows * fanout, experts)
    earlier = jnp.cumsum(onehot, axis=1) - onehot
    within = jnp.sum(earlier * onehot, axis=-1).reshape(chosen.shape)
    heading = lax.broadcasted_iota(jnp.int32, chosen.shape, 0)
    member = lax.broadcasted_iota(jnp.int32, chosen.shape, 1)
    target = chosen * (2 * capacity) + heading * capacity + within
    anchor = heading * tok_rows + member
    owner = (
        jnp.full((experts * 2 * capacity,), 2 * tok_rows, jnp.int32)
        .at[target.reshape(-1)]
        .set(anchor.reshape(-1))
    )
    hidden = normed.astype(jnp.bfloat16).reshape(2 * tok_rows, quarter)
    table = jnp.concatenate([hidden, jnp.zeros((1, quarter), jnp.bfloat16)], axis=0)
    outgoing = table[owner].reshape(experts, 2 * capacity, quarter)
    upper = w_up[0]
    lower = w_down[0]
    received = lax.all_to_all(outgoing, "expert", split_axis=0, concat_axis=0, tiled=True)
    senders = received.shape[0]
    count = received.shape[1]
    inner = jnp.dot(received.reshape(-1, quarter), upper, preferred_element_type=jnp.float32)
    share = lax.psum_scatter(inner, "tensor", scatter_dimension=1, tiled=True)
    active = lax.all_gather(jax.nn.silu(share).astype(jnp.bfloat16), "tensor", axis=1, tiled=True)
    produced = jnp.dot(active, lower, preferred_element_type=jnp.float32).astype(jnp.bfloat16)
    answers = lax.all_to_all(
        produced.reshape(senders, count, quarter), "expert", split_axis=0, concat_axis=0, tiled=True
    )
    flat_back = answers.reshape(experts * 2 * capacity, quarter)
    gathered = (
        flat_back[target.reshape(-1)].reshape(2, tok_rows, fanout, quarter).astype(jnp.float32)
    )
    mixed = jnp.einsum("dtk,dtkc->dtc", gates, gathered)
    result = (arrived + mixed).astype(jnp.bfloat16)
    return result[:, None]


def solution(mesh):
    return jax.shard_map(
        shards,
        mesh=mesh,
        in_specs=(
            P(None, "pipe", "expert", "tensor"),
            P(None, "pipe", "expert", None),
            P("pipe", "tensor"),
            P("pipe", "tensor", None),
            P("expert", "tensor", None),
            P("expert", None, "tensor"),
        ),
        out_specs=P(None, "pipe", "expert", "tensor"),
        check_vma=False,
    )
```

profile of v0, /device:TPU:0, one launch (start us, length us, event | category | flops | bytes accessed | tf_op | source)
XLA Modules:
  0.0 101.9 jit_solution(15306226972587400173)
XLA Ops:
  6.5 0.0 copy-start
  6.5 0.0 reduce-scatter.2.cloned.1.call-start
  6.5 1.0 slice_bitcast_fusion.1
  7.5 0.5 collective-permute-start
  8.1 2.0 %collective-permute-start.1 = (bf16[1,16,3584]{2,1,0:T(8,128)(2,1)S(1)}, bf16[1,16,3584]{2,1,0:T(8,128)(2,1)S(1)}, u32[]{:S(2)}, u32[]{:S(2)}) collective-permute-start(bf16[1,16,3584]{2,1,0:T(8,128)(2,1)S(1)} %get-tuple-element.8), channel_id=1, source_target_pairs={{0,24},{8,0},{16,8},{24,16},{1,25},{9,1},{17,9},{25,17},{2,26},{10... | collective-permute-start | bytes 344072 | tf_op jit(solution)/shard_map/ppermute | solution.py:12
  10.0 0.8 copy.14
  10.8 0.7 broadcast_multiply_fusion
  11.5 0.1 eq.16
  11.6 0.1 fusion.18
  11.7 0.1 reduce_window_sum.11
  11.7 0.2 select_reduce_fusion
  11.9 0.1 reshape.116
  12.0 0.1 copy.13
  12.1 0.1 mul.92
  12.2 0.1 iota.24
  12.3 0.1 iota.25
  12.4 0.1 iota_add_fusion
  12.5 0.1 reshape.149
  12.6 0.8 scatter_custom_fusion
  13.4 0.8 reduce
  14.1 0.0 collective-permute-done
  14.2 0.0 collective-permute-done.1
  14.2 0.1 multiply_reduce_fusion
  14.3 5.2 %psum.14 = f32[2,16]{1,0:T(2,128)S(1)} all-reduce(f32[2,16]{1,0:T(2,128)S(1)} %multiply_reduce_fusion), channel_id=1, replica_groups=mesh['pipe'=4,'expert'=4,'tensor'=2] {'tensor'}, use_global_device_ids=true, to_apply=%region_1.0 | all-reduce | flops 32 | bytes 256 | tf_op jit(solution)/shard_map/psum | solution.py:25
  19.5 0.1 mul.87
  19.6 0.1 fusion.9
  19.7 1.0 gather_fusion
  20.7 22.2 %all_to_all.10 = bf16[4,24,3584]{2,1,0:T(8,128)(2,1)S(1)} all-to-all(bf16[4,24,3584]{2,1,0:T(8,128)(2,1)S(1)} %bitcast.63), channel_id=1, replica_groups=mesh['pipe'=4,'expert'=4,'tensor'=2] {'expert'}, dimensions={0} | all-to-all | bytes 1376256 | tf_op jit(solution)/shard_map/all_to_all | solution.py:54
  42.8 5.1 %fusion.2 = f32[96,1024]{1,0:T(8,128)} fusion(bf16[96,3584]{1,0:T(8,128)(2,1)S(1)} %bitcast.62, bf16[1,3584,1024]{2,1,0:T(8,128)(2,1)} %param.10), kind=kOutput, calls=%fused_computation.6 | convolution fusion | flops 704643072 | bytes 8421376 | tf_op jit(solution)/shard_map/dot_general | solution.py:57
  47.9 0.0 reduce-scatter.2.cloned.1.call-update
  48.0 11.9 %reduce-scatter.2.cloned.1.call-done = f32[96,512]{1,0:T(8,128)} async-done(((f32[96,1024]{1,0:T(8,128)}), f32[96,512]{1,0:T(8,128)}) %reduce-scatter.2.cloned.1.call-update) | async-done | bytes 196624 | tf_op jit(solution)/shard_map/reduce_scatter | solution.py:58
  59.9 1.0 multiply_convert_fusion
  60.9 5.3 %all_gather.3 = bf16[96,1024]{1,0:T(8,128)(2,1)S(1)} all-gather(bf16[96,512]{1,0:T(8,128)(2,1)S(1)} %multiply_convert_fusion), channel_id=1, replica_groups=mesh['pipe'=4,'expert'=4,'tensor'=2] {'tensor'}, dimensions={1}, use_global_device_ids=true | all-gather | bytes 294912 | tf_op jit(solution)/shard_map/all_gather | solution.py:59
  66.1 5.2 %fusion.4 = bf16[96,3584]{1,0:T(8,128)(2,1)} fusion(bf16[96,1024]{1,0:T(8,128)(2,1)S(1)} %all_gather.3, bf16[1,1024,3584]{2,1,0:T(8,128)(2,1)} %param.11), kind=kOutput, calls=%fused_computation.8 | convolution fusion | flops 704987136 | bytes 8224768 | tf_op jit(solution)/shard_map/dot_general | solution.py:60
  71.4 4.6 %all-to-all-start.1 = ((bf16[4,24,3584]{2,1,0:T(8,128)(2,1)}), bf16[4,24,3584]{2,1,0:T(8,128)(2,1)S(1)}, u32[]{:S(2)}, u32[]{:S(2)}) async-start(bf16[4,24,3584]{2,1,0:T(8,128)(2,1)} %bitcast.13), calls=%async_computation.2 | async-start | bytes 1376256 | tf_op jit(solution)/shard_map/all_to_all | solution.py:61
  76.0 0.1 copy.11
  76.1 0.1 reshape.139
  76.2 1.8 %fusion.10 = f32[2,16,4]{1,2,0:T(4,128)S(1)} fusion(f32[2,16]{1,0:T(2,128)S(1)} %add_rsqrt_fusion, f32[3584]{0:T(1024)S(1)} %reduce, f32[1,3584,4]{1,2,0:T(4,128)S(1)} %copy-done, bf16[1,16,3584]{2,1,0:T(8,128)(2,1)S(1)} %collective-permute-done.1, bf16[1,16,3584]{2,1,0:T(8,128)(2,1)S(1)} %collective-permute-done), kind=kOutput, calls=%fused_computation.14 | convolution fusion | flops 5963776 | bytes 301696 | tf_op jit(solution)/shard_map/dtc,ce->dte/dot_general | solution.py:28
  78.0 4.9 %psum.15 = f32[2,16,4]{1,2,0:T(4,128)S(1)} all-reduce(f32[2,16,4]{1,2,0:T(4,128)S(1)} %fusion.10), channel_id=1, replica_groups=mesh['pipe'=4,'expert'=4,'tensor'=2] {'tensor'}, use_global_device_ids=true, to_apply=%region_2.0 | all-reduce | flops 128 | bytes 1024 | tf_op jit(solution)/shard_map/psum | solution.py:28
  82.9 1.0 gather_fusion.2
  83.9 0.1 reshape.142
  84.0 0.1 copy.12
  84.2 0.1 copy.15
  84.3 8.4 %all-to-all-done.1 = bf16[4,24,3584]{2,1,0:T(8,128)(2,1)S(1)} async-done(((bf16[4,24,3584]{2,1,0:T(8,128)(2,1)}), bf16[4,24,3584]{2,1,0:T(8,128)(2,1)S(1)}, u32[]{:S(2)}, u32[]{:S(2)}) %all-to-all-start.1) | async-done | bytes 688160 | tf_op jit(solution)/shard_map/all_to_all | solution.py:61
  92.7 0.8 gather_fusion.1
  93.5 0.2 reshape.121
  93.7 0.6 fusion.27
  94.3 0.7 fusion.14
  (14 shorter events, 0.1 us)
Async XLA Ops:
  6.5 69.7 %copy-start = (f32[1,3584,4]{1,2,0:T(4,128)S(1)}, f32[1,3584,4]{1,2,0:T(4,128)}, u32[]{:S(2)}) copy-start(f32[1,3584,4]{1,2,0:T(4,128)} %param.9) | copy-start | bytes 172036
  6.5 53.3 %reduce-scatter.2.cloned.1.call-start = ((), (), s32[]{:S(2)}) async-start(), calls=%async_computation.3 | async-start | bytes 589824 | tf_op jit(solution)/shard_map/reduce_scatter | solution.py:58
  7.5 6.6 %collective-permute-start = (bf16[1,16,3584]{2,1,0:T(8,128)(2,1)S(1)}, bf16[1,16,3584]{2,1,0:T(8,128)(2,1)S(1)}, u32[]{:S(2)}, u32[]{:S(2)}) collective-permute-start(bf16[1,16,3584]{2,1,0:T(8,128)(2,1)S(1)} %get-tuple-element.7), channel_id=1, source_target_pairs={{0,8},{8,16},{16,24},{24,0},{1,9},{9,17},{17,25},{25,1},{2,10},{10... | collective-permute-start | bytes 344072 | tf_op jit(solution)/shard_map/ppermute | solution.py:12
  8.1 6.1 %collective-permute-start.1 = (bf16[1,16,3584]{2,1,0:T(8,128)(2,1)S(1)}, bf16[1,16,3584]{2,1,0:T(8,128)(2,1)S(1)}, u32[]{:S(2)}, u32[]{:S(2)}) collective-permute-start(bf16[1,16,3584]{2,1,0:T(8,128)(2,1)S(1)} %get-tuple-element.8), channel_id=1, source_target_pairs={{0,24},{8,0},{16,8},{24,16},{1,25},{9,1},{17,9},{25,17},{2,26},{10... | collective-permute-start | bytes 344072 | tf_op jit(solution)/shard_map/ppermute | solution.py:12
  66.1 9.9 %copy-start.1 = (s32[2,1,16,2]{2,3,1,0:T(2,128)S(1)}, s32[2,1,16,2]{2,3,1,0:T(2,128)}, u32[]{:S(2)}) copy-start(s32[2,1,16,2]{2,3,1,0:T(2,128)} %param.7) | copy-start | bytes 772
  71.4 21.3 %all-to-all-start.1 = ((bf16[4,24,3584]{2,1,0:T(8,128)(2,1)}), bf16[4,24,3584]{2,1,0:T(8,128)(2,1)S(1)}, u32[]{:S(2)}, u32[]{:S(2)}) async-start(bf16[4,24,3584]{2,1,0:T(8,128)(2,1)} %bitcast.13), calls=%async_computation.2 | async-start | bytes 1376256 | tf_op jit(solution)/shard_map/all_to_all | solution.py:61
Sparse Core Ops, SparseCore 0:
  48.1 11.7 reduce-scatter.1
where the time goes:
time: 102 us
  blocking collectives  37.5 us (37%)
  waiting for transfers between devices  20.3 us (20%)
  between operations  13.6 us (13%)
  matrix products  12.8 us (13%)
  starting transfers between devices  7.13 us (7%)
  local copies, waits for them, and re-layouts  6.7 us (7%)
  other arithmetic  3.87 us (4%)
    all_to_all x1, blocking collectives, shards(): lax.all_to_all(outgoing, 'expert', split_axis=0, concat_axis=0, tiled=True)  22.2 us
    reduce_scatter x1, waiting for transfers between devices, shards(): share = lax.psum_scatter(inner, 'tensor', scatter_dimension=1, tiled=True)  11.9 us
    all_to_all x1, waiting for transfers between devices, shards(): lax.all_to_all(produced.reshape(senders, count, quarter), 'expert', split...  8.42 us
    all_gather x1, blocking collectives, shards(): lax.all_gather(jax.nn.silu(share).astype(jnp.bfloat16), 'tensor', axis=1,...  5.29 us
    dot_general x1, matrix products, shards(): jnp.dot(active, lower, preferred_element_type=jnp.float32)  5.25 us
    psum x1, blocking collectives, shards(): total_sq = lax.psum(squares, 'tensor')  5.16 us
    dot_general x1, matrix products, shards(): jnp.dot(received.reshape(-1, quarter), upper, preferred_element_type=jnp....  5.11 us
    psum x1, blocking collectives, shards(): lax.psum(jnp.einsum('dtc,ce->dte', normed, router[0], precision=highest),...  4.93 us
  transfers between devices with their start and end apart: 4, of which 2 were waited for; matrix products, arithmetic and copies ran while one was open for 7% of the time, Pallas kernels for 0%

commit v1 on v0

v1 whole, which is shorter than its diff:
```python
import functools

import jax
import jax.numpy as jnp
from jax import lax
from jax.experimental import pallas as pl
from jax.experimental.pallas import tpu as pltpu
from jax.sharding import PartitionSpec as P

norm_eps = 1e-06
route_scale = 2.5
MESH = pl.DeviceIdType.MESH


def pieces_of(width, most):
    for count in range(most, 0, -1):
        if width % (count * 128) == 0:
            return count
    return 1


def layer(
    sizes, slots, feat, cols,
    stream, ids_ref, gain_hbm, router_ref, up_hbm, down_hbm, out_ref,
    up, down, arrived, send, recv, rows32, inner, part, parts_in, active, squares, squares_in,
    small, small_in, ret, back, weights, gain_ref,
    load_sem, shift_send, shift_recv, disp_send, disp_recv, ten_send, ten_recv, ret_send, ret_recv,
):
    n_pipe, n_exp, n_ten = sizes
    pipe, expert, tensor = lax.axis_index("pipe"), lax.axis_index("expert"), lax.axis_index("tensor")
    tokens, width = arrived.shape
    half = tokens // 2
    hidden_units = up.shape[1]
    experts = router_ref.shape[0]
    step_f, step_c = width // feat, hidden_units // cols

    def section(by):
        return (lax.rem(pipe + by + n_pipe, n_pipe), expert, tensor)

    def member(by):
        return (pipe, lax.rem(expert + by + n_exp, n_exp), tensor)

    def holder(by):
        return (pipe, expert, lax.rem(tensor + by + n_ten, n_ten))

    barrier = pltpu.get_barrier_semaphore()
    greeted = [section(1), section(-1)]
    greeted += [member(o) for o in range(1, n_exp)] + [holder(o) for o in range(1, n_ten)]
    for who in greeted:
        pl.semaphore_signal(barrier, inc=1, device_id=who, device_id_type=MESH)

    loads = []
    for f in range(feat):
        at = pl.ds(f * step_f, step_f)
        loads.append(pltpu.make_async_copy(up_hbm.at[0, at], up.at[at], load_sem.at[f]))
    loads.append(pltpu.make_async_copy(down_hbm.at[0], down, load_sem.at[feat]))
    gain_load = pltpu.make_async_copy(
        gain_hbm, gain_ref.at[:, pl.ds(0, width)], load_sem.at[feat + 1]
    )
    gain_load.start()
    for load in loads:
        load.start()
    pl.semaphore_wait(barrier, len(greeted))

    shifts = [
        pltpu.make_async_remote_copy(
            src_ref=stream.at[d, 0], dst_ref=arrived.at[pl.ds(d * half, half)],
            send_sem=shift_send.at[d], recv_sem=shift_recv.at[d],
            device_id=section(1 - 2 * d), device_id_type=MESH,
        )
        for d in range(2)
    ]
    for copy in shifts:
        copy.start()

    ids = ids_ref[...]
    total = n_exp * slots
    lane = lax.broadcasted_iota(jnp.int32, (tokens, total), 1)
    block = lane // slots
    lane_expert = lax.rem(block + expert, n_exp)
    takes = jnp.zeros((tokens, total), jnp.float32)
    for k in range(ids.shape[1]):
        takes += jnp.where(ids[:, k : k + 1] == lane_expert, 1.0, 0.0)
    below = lax.broadcasted_iota(jnp.int32, (tokens, tokens), 0) > lax.broadcasted_iota(
        jnp.int32, (tokens, tokens), 1
    )
    rank = jnp.dot(
        jnp.where(below, 1.0, 0.0).astype(jnp.bfloat16),
        takes.astype(jnp.bfloat16),
        preferred_element_type=jnp.float32,
    )
    spot = (lane - block * slots).astype(jnp.float32)
    place = jnp.where((rank == spot) & (takes > 0.0), 1.0, 0.0)
    pick = place.astype(jnp.bfloat16)

    for copy in shifts:
        copy.wait_recv()

    dispatch = {}
    for f in range(feat):
        at = pl.ds(f * step_f, step_f)
        taken = lax.dot_general(
            pick, arrived[:, at], (((0,), (0,)), ((), ())), preferred_element_type=jnp.float32
        ).astype(jnp.float32)
        for o in list(range(1, n_exp)) + [0]:
            rows = taken[o * slots : (o + 1) * slots].astype(jnp.bfloat16)
            if o == 0:
                recv[0, 0:slots, at] = rows
                continue
            send[o, 0:slots, at] = rows
            dispatch[o, f] = pltpu.make_async_remote_copy(
                src_ref=send.at[o, pl.ds(0, slots), at], dst_ref=recv.at[o, pl.ds(0, slots), at],
                send_sem=disp_send.at[o, f], recv_sem=disp_recv.at[o, f],
                device_id=member(o), device_id_type=MESH,
            )
            dispatch[o, f].start()

    gain_load.wait()
    held = arrived[...].astype(jnp.float32)
    small[0] = jnp.broadcast_to(jnp.sum(held * held, axis=1, keepdims=True), (tokens, 128))
    small[1] = jnp.zeros((tokens, 128), jnp.float32)
    small[1, :, 0:experts] = lax.dot_general(
        held * gain_ref[:, 0:width], router_ref[...], (((1,), (1,)), ((), ())),
        preferred_element_type=jnp.float32, precision=lax.Precision.HIGHEST,
    )

    def to_holders(src, dst, sem):
        copies = [
            pltpu.make_async_remote_copy(
                src_ref=src, dst_ref=dst(o), send_sem=ten_send.at[o, sem], recv_sem=ten_recv.at[o, sem],
                device_id=holder(o), device_id_type=MESH,
            )
            for o in range(1, n_ten)
        ]
        for copy in copies:
            copy.start()
        return copies

    small_copies = to_holders(small, lambda o: small_in.at[o], cols)

    square = jnp.zeros((total, 1), jnp.float32)
    for f in range(feat):
        at = pl.ds(f * step_f, step_f)
        gain = gain_ref[:, at]
        for o in range(n_exp):
            if o > 0:
                dispatch[o, f].wait_recv()
            rows32[pl.ds(o * slots, slots), :] = recv[o, 0:slots, at].astype(jnp.float32)
        rows = rows32[...]
        square += jnp.sum(rows * rows, axis=1, keepdims=True)
        if f == feat - 1:
            squares[...] = jnp.broadcast_to(square, (total, 128))
            square_copies = to_holders(squares, lambda o: squares_in.at[o], cols + 1)
        lifted = (rows * gain).astype(jnp.bfloat16)
        loads[f].wait()
        if f < feat - 1:
            found = jnp.dot(lifted, up[at, :], preferred_element_type=jnp.float32)
            if f == 0:
                inner[...] = found
            else:
                inner[...] += found
    exchange = []
    for c in range(cols):
        units = pl.ds(c * step_c, step_c)
        found = jnp.dot(lifted, up[at, units], preferred_element_type=jnp.float32)
        if feat > 1:
            found += inner[:, units]
        inner[:, units] = found
        part[c] = found.astype(jnp.bfloat16)
        exchange.append(to_holders(part.at[c], lambda o, c=c: parts_in.at[o, c], c))

    for copy in small_copies:
        copy.wait_recv()
    sums, logits = small[0], small[1, :, 0:experts]
    for o in range(1, n_ten):
        sums = sums + small_in[o, 0]
        logits = logits + small_in[o, 1, :, 0:experts]
    full = float(width * n_ten)
    logits = logits * lax.rsqrt(sums[:, 0:1] / full + norm_eps)
    which = lax.broadcasted_iota(jnp.int32, logits.shape, 1)
    scores = []
    for k in range(ids.shape[1]):
        picked = jnp.sum(jnp.where(ids[:, k : k + 1] == which, logits, 0.0), axis=1, keepdims=True)
        scores.append(1.0 / (1.0 + jnp.exp(-picked)))
    norm = scores[0]
    for score in scores[1:]:
        norm = norm + score
    gate = jnp.zeros((tokens, total), jnp.float32)
    for k, score in enumerate(scores):
        gate += jnp.where(ids[:, k : k + 1] == lane_expert, route_scale * score / norm, 0.0)
    gate = gate * place
    coarse = gate.astype(jnp.bfloat16)
    weights[0, :, 0:total] = coarse
    weights[1, :, 0:total] = (gate - coarse.astype(jnp.float32)).astype(jnp.bfloat16)

    for copy in square_copies:
        copy.wait_recv()
    total_sq = squares[...]
    for o in range(1, n_ten):
        total_sq = total_sq + squares_in[o]
    inverse = lax.rsqrt(total_sq[:, 0:1] / full + norm_eps)
    for c in range(cols):
        units = pl.ds(c * step_c, step_c)
        for copy in exchange[c]:
            copy.wait_recv()
        value = inner[:, units]
        for o in range(1, n_ten):
            value = value + parts_in[o, c].astype(jnp.float32)
        value = value * inverse
        active[:, units] = (value / (1.0 + jnp.exp(-value))).astype(jnp.bfloat16)

    loads[feat].wait()
    returns = {}
    for f in range(feat):
        at = pl.ds(f * step_f, step_f)
        made = jnp.dot(active[...], down[:, at], preferred_element_type=jnp.float32)
        for o in list(range(1, n_exp)) + [0]:
            rows = made[o * slots : (o + 1) * slots].astype(jnp.bfloat16)
            if o == 0:
                back[0, 0:slots, at] = rows
                continue
            ret[o, 0:slots, at] = rows
            returns[o, f] = pltpu.make_async_remote_copy(
                src_ref=ret.at[o, pl.ds(0, slots), at], dst_ref=back.at[o, pl.ds(0, slots), at],
                send_sem=ret_send.at[o, f], recv_sem=ret_recv.at[o, f],
                device_id=member(-o), device_id_type=MESH,
            )
            returns[o, f].start()

    for f in range(feat):
        at = pl.ds(f * step_f, step_f)
        for o in range(n_exp):
            if o > 0:
                returns[o, f].wait_recv()
            rows32[pl.ds(o * slots, slots), :] = back[o, 0:slots, at].astype(jnp.float32)
        rows = rows32[...].astype(jnp.bfloat16)
        mixed = jnp.dot(weights[0, :, 0:total], rows, preferred_element_type=jnp.float32)
        mixed += jnp.dot(weights[1, :, 0:total], rows, preferred_element_type=jnp.float32)
        out_ref[:, at] = (arrived[:, at].astype(jnp.float32) + mixed).astype(jnp.bfloat16)

    for copies in [shifts, dispatch.values(), small_copies, square_copies, returns.values()] + exchange:
        for copy in copies:
            copy.wait_send()


def shards(sizes, stream, expert_ids, norm_gain, router, w_up, w_down):
    n_pipe, n_exp, n_ten = sizes
    tok_rows, width = stream.shape[2:]
    fanout = expert_ids.shape[-1]
    experts = router.shape[2]
    hidden_units = w_up.shape[2]
    tokens = 2 * tok_rows
    capacity = 3 * tok_rows * fanout // (2 * experts)
    slots = -(-2 * capacity // 8) * 8
    total = n_exp * slots
    feat = pieces_of(width, 4)
    cols = pieces_of(hidden_units, 4)
    bf16, f32 = jnp.bfloat16, jnp.float32
    dma = pltpu.SemaphoreType.DMA
    vmem = pl.BlockSpec(memory_space=pltpu.VMEM)
    hbm = pl.BlockSpec(memory_space=pl.ANY)
    result = pl.pallas_call(
        functools.partial(layer, sizes, slots, feat, cols),
        out_shape=jax.ShapeDtypeStruct((tokens, width), bf16),
        in_specs=[hbm, vmem, hbm, vmem, hbm, hbm],
        out_specs=vmem,
        scratch_shapes=[
            pltpu.VMEM((width, hidden_units), bf16),
            pltpu.VMEM((hidden_units, width), bf16),
            pltpu.VMEM((tokens, width), bf16),
            pltpu.VMEM((n_exp, -(-slots // 16) * 16, width), bf16),
            pltpu.VMEM((n_exp, -(-slots // 16) * 16, width), bf16),
            pltpu.VMEM((total, width // feat), f32),
            pltpu.VMEM((total, hidden_units), f32),
            pltpu.VMEM((cols, total, hidden_units // cols), bf16),
            pltpu.VMEM((n_ten, cols, total, hidden_units // cols), bf16),
            pltpu.VMEM((total, hidden_units), bf16),
            pltpu.VMEM((total, 128), f32),
            pltpu.VMEM((n_ten, total, 128), f32),
            pltpu.VMEM((2, tokens, 128), f32),
            pltpu.VMEM((n_ten, 2, tokens, 128), f32),
            pltpu.VMEM((n_exp, -(-slots // 16) * 16, width), bf16),
            pltpu.VMEM((n_exp, -(-slots // 16) * 16, width), bf16),
            pltpu.VMEM((2, tokens, -(-total // 128) * 128), bf16),
            pltpu.VMEM((1, width + 1024), f32),
            dma((feat + 2,)),
            dma((2,)),
            dma((2,)),
            dma((n_exp, feat)),
            dma((n_exp, feat)),
            dma((n_ten, cols + 2)),
            dma((n_ten, cols + 2)),
            dma((n_exp, feat)),
            dma((n_exp, feat)),
        ],
        compiler_params=pltpu.CompilerParams(
            collective_id=0, has_side_effects=True, vmem_limit_bytes=60 * 1024 * 1024
        ),
    )(stream, expert_ids.reshape(tokens, fanout), norm_gain, router[0].T, w_up, w_down)
    return result.reshape(2, 1, tok_rows, width)


def solution(mesh):
    sizes = tuple(mesh.shape[axis] for axis in ("pipe", "expert", "tensor"))
    return jax.shard_map(
        functools.partial(shards, sizes),
        mesh=mesh,
        in_specs=(
            P(None, "pipe", "expert", "tensor"),
            P(None, "pipe", "expert", None),
            P("pipe", "tensor"),
            P("pipe", "tensor", None),
            P("expert", "tensor", None),
            P("expert", None, "tensor"),
        ),
        out_specs=P(None, "pipe", "expert", "tensor"),
        check_vma=False,
    )
```

time: 102 us -> 56 us (0.55)
  Pallas kernels: 0 us -> 52.7 us
  blocking collectives: 37.5 us -> 0 us
  waiting for transfers between devices: 20.3 us -> 0 us
  between operations: 13.6 us -> 0.01 us
  matrix products: 12.8 us -> 0 us
  starting transfers between devices: 7.13 us -> 0 us
  other arithmetic: 3.87 us -> 0 us
  local copies, waits for them, and re-layouts: 6.7 us -> 3.01 us
    pallas_call x0 -> x1, Pallas kernels: none -> 52.7 us  [shards(): pl.pallas_call(functools.partial(layer, sizes, slots, feat, cols), out_sh...]
    all_to_all x1 -> x0, blocking collectives: 22.2 us -> none  [shards(): lax.all_to_all(outgoing, 'expert', split_axis=0, concat_axis=0, tiled=True)]
    dot_general x4 -> x0, matrix products: 12.8 us -> none  [the longest x1 5.25 us: shards(): jnp.dot(active, lower, preferred_element_type=jnp.float32)]
    reduce_scatter x1 -> x0, waiting for transfers between devices: 11.9 us -> none  [shards(): share = lax.psum_scatter(inner, 'tensor', scatter_dimension=1, tiled=True)]
    psum x2 -> x0, blocking collectives: 10.1 us -> none  [the longest x1 5.16 us: shards(): total_sq = lax.psum(squares, 'tensor')]
    all_to_all x1 -> x0, waiting for transfers between devices: 8.42 us -> none  [shards(): lax.all_to_all(produced.reshape(senders, count, quarter), 'expert', split...]
    all_gather x1 -> x0, blocking collectives: 5.29 us -> none  [shards(): lax.all_gather(jax.nn.silu(share).astype(jnp.bfloat16), 'tensor', axis=1,...]
    all_to_all x1 -> x0, starting transfers between devices: 4.61 us -> none  [shards(): lax.all_to_all(produced.reshape(senders, count, quarter), 'expert', split...]
  transfers between devices with their start and end apart: 4 -> 0, of which waited for: 2 -> 0; matrix products, arithmetic and copies ran while one was open for 7% -> 0% of each run, Pallas kernels for 0% -> 0%
where the time goes in v1:
time: 56 us; the launch traced here: 55.8 us
  Pallas kernels  52.7 us (94%)
  local copies, waits for them, and re-layouts  3.01 us (5%)
    pallas_call x1, Pallas kernels, shards(): pl.pallas_call(functools.partial(layer, sizes, slots, feat, cols), out_sh...  52.7 us
    unnamed x1, local copies, waits for them, and re-layouts  1.64 us
    reshape x1, local copies, waits for them, and re-layouts, shards(): expert_ids.reshape(tokens, fanout)  1.37 us

profile of v1, /device:TPU:0, one launch (start us, length us, event | category | flops | bytes accessed | tf_op | source)
XLA Modules:
  0.0 55.8 jit_solution(2057308630672818085)
XLA Ops:
  0.0 1.4 %copy.10 = s32[2,1,16,2]{3,2,0,1:T(8,128)} copy(s32[2,1,16,2]{2,3,1,0:T(2,128)} %param.7) | data formatting | bytes 512 | tf_op jit(solution)/shard_map/reshape | solution.py:299
  1.4 52.7 %shard_map.64 = bf16[32,3584]{1,0:T(8,128)(2,1)} custom-call(bf16[2,1,16,3584]{3,2,1,0:T(8,128)(2,1)} %stream.1, s32[32,2]{1,0:T(8,128)} %bitcast.8, f32[1,3584]{1,0:T(1,128)} %gain_hbm.1, f32[4,3584]{1,0:T(4,128)} %bitcast.9, bf16[1,3584,1024]{2,1,0:T(8,128)(2,1)} %up_hbm.1, bf16[1,1024,3584]{2,1,0:T(8,128)(2,1)} %down_hbm.1), custom_call_target="tpu_custom_call" | custom-call | tf_op jit(solution)/shard_map/pallas_call | solution.py:262
  54.1 1.6 %copy.13 = bf16[2,1,16,3584]{3,2,1,0:T(8,128)(2,1)} copy(bf16[2,1,16,3584]{3,2,1,0:T(8,128)(2,1)} %bitcast.7) | data formatting | bytes 458752
